TPU v7x, 32 devices: a whole 2x2x4 slice. The times are simulated.
32 devices in a mesh: slab: 4 (over y, core), inner: 8 (over z, x).
Axes of the slice: x: 2, y: 2, z: 4, core: 2. Of those that a mesh axis runs over, the one named last changes fastest.
Arguments:
- x_in: bfloat16 [8192, 16384], P(('slab', 'inner')), may hold values from -6 to 6
- bc_in: bfloat16 [8192, 4096], P(('slab', 'inner')), may hold values from -6 to 6
- dt_raw: bfloat16 [8192, 256], P(('slab', 'inner')), may hold values from -6.7 to -4.3
- dt_bias: float32 [256], replicated, may hold values from -0.5 to 0.5
- a_log: float32 [256], replicated, may hold values from -8 to 0, as said below
- d_skip: float32 [256], replicated, may hold values from 0.5 to 1.5
- conv_x_weight: float32 [4, 16384], replicated, may hold values from -3 to 3
- conv_x_bias: float32 [16384], replicated, may hold values from -3 to 3
- conv_bc_weight: float32 [4, 4096], replicated, may hold values from -3 to 3
- conv_bc_bias: float32 [4096], replicated, may hold values from -3 to 3
Outputs:
- y_out: bfloat16 [8192, 16384], P('slab', 'inner')
Inputs may be any that keep to these rules, and one draw needn't show every extreme that they name: `a_log`: per-head logarithm of the decay rate.
All inputs are finite; a program needn't handle non-finite values.
Results may differ from a plain program's by a relative error of at most 0.0034.
Values may be sent and summed in bfloat16 or wider, within the bound.
No kernel may reach another device: no remote copies, remote signals or barrier semaphores. Data moves between devices by JAX's collectives and lax.ppermute only.
A program may use at most 256 MiB of HBM per device.

v0:
```python
import jax
import jax.numpy as jnp
import numpy as np
from jax import lax
from jax.sharding import PartitionSpec as P

HEADS = 256
HEADDIM = 64
STATE = 256
GROUPS = 8
CONV = 4
SPAN = 256


def from_behind(x, axis, by):
    size = lax.axis_size(axis)
    pairs = [(i, i + by) for i in range(size) if 0 <= i + by < size]
    return lax.ppermute(x, axis, pairs)


def causal_conv(row_block, before, weight, conv_bias):
    kernel_len = weight.shape[0]
    length = row_block.shape[0]
    padded = jnp.concatenate([before, row_block], axis=0).astype(jnp.float32)
    summed = conv_bias[None, :] + weight[0][None, :] * padded[0:length]
    for offset in range(1, kernel_len):
        summed = summed + weight[offset][None, :] * padded[offset : offset + length]
    return jax.nn.silu(summed).astype(jnp.bfloat16)


def head_columns(per_head, head_count):
    rows = per_head.shape[0]
    return jnp.broadcast_to(per_head[:, :, None], (rows, head_count, HEADDIM)).reshape(
        rows, head_count * HEADDIM
    )


def span_step(state, pieces):
    x_span, b_span, c_span, dt_span, da_span = pieces
    size_q = x_span.shape[0]
    head_count = dt_span.shape[1]
    cumul = jnp.cumsum(da_span, axis=0).T
    row_ids = lax.broadcasted_iota(jnp.int32, (size_q, size_q), 0)
    col_ids = lax.broadcasted_iota(jnp.int32, (size_q, size_q), 1)
    gaps = cumul[:, :, None] - cumul[:, None, :]
    decays = jnp.where((row_ids >= col_ids)[None], jnp.exp(jnp.minimum(gaps, 0.0)), 0.0)
    scores = jnp.dot(c_span, b_span.T, preferred_element_type=jnp.float32)
    mixing = (decays * scores[None] * dt_span.T[:, None, :]).astype(jnp.bfloat16)
    x_heads = x_span.reshape(size_q, head_count, HEADDIM)
    y_intra = jnp.einsum(
        "hts,shp->thp", mixing, x_heads, preferred_element_type=jnp.float32
    ).reshape(size_q, head_count * HEADDIM)
    y_inter = jnp.dot(c_span, state.astype(jnp.bfloat16), preferred_element_type=jnp.float32)
    y_inter = y_inter * head_columns(jnp.exp(cumul.T), head_count)
    weights_end = (jnp.exp(cumul[:, -1:] - cumul) * dt_span.T).T
    scaled = (x_span.astype(jnp.float32) * head_columns(weights_end, head_count)).astype(
        jnp.bfloat16
    )
    contrib = jnp.dot(b_span.T, scaled, preferred_element_type=jnp.float32)
    end_decay = head_columns(jnp.exp(cumul[:, -1])[None, :], head_count)
    new_state = end_decay * state + contrib
    return (new_state, y_intra + y_inter)


def slab_core(x_rows, b_rows, c_rows, dt_rows, da_rows):
    length = x_rows.shape[0]
    width = x_rows.shape[1]
    head_count = dt_rows.shape[1]
    span_count = length // SPAN
    inputs = (
        x_rows.reshape(span_count, SPAN, width),
        b_rows.reshape(span_count, SPAN, STATE),
        c_rows.reshape(span_count, SPAN, STATE),
        dt_rows.reshape(span_count, SPAN, head_count),
        da_rows.reshape(span_count, SPAN, head_count),
    )
    zero_state = jnp.zeros((STATE, width), jnp.float32)
    end_state, outputs = lax.scan(span_step, zero_state, inputs)
    return (outputs.reshape(length, width), end_state)


def group_copies(bc_rows, dest_group, n_inner):
    tok_rows = bc_rows.shape[0]
    split = bc_rows.reshape(tok_rows, 2, GROUPS, STATE)
    picked = jnp.take(split, dest_group, axis=2)
    return jnp.transpose(picked, (0, 2, 1, 3)).reshape(tok_rows, n_inner, 2 * STATE)


def shards(
    x_in,
    bc_in,
    dt_raw,
    dt_bias,
    a_log,
    d_skip,
    conv_x_weight,
    conv_x_bias,
    conv_bc_weight,
    conv_bc_bias,
):
    n_inner = lax.axis_size("inner")
    n_slab = lax.axis_size("slab")
    tok_dev = x_in.shape[0]
    heads_dev = HEADS // n_inner
    ch_dev = heads_dev * HEADDIM
    per_group = HEADS // GROUPS
    inner_idx = lax.axis_index("inner")
    dest_group = np.arange(n_inner) * heads_dev // per_group
    edge = CONV - 1
    dt_send = dt_raw.reshape(tok_dev, n_inner, heads_dev)
    x_prev, bc_prev = from_behind(
        (x_in[tok_dev - edge :], bc_in[tok_dev - edge :]), ("slab", "inner"), 1
    )
    x_ready = causal_conv(x_in, x_prev, conv_x_weight, conv_x_bias)
    bc_ready = causal_conv(bc_in, bc_prev, conv_bc_weight, conv_bc_bias)
    bc_send = group_copies(bc_ready, dest_group, n_inner)
    x_recv, bc_recv, dt_recv = (
        lax.all_to_all(
            x_ready.reshape(tok_dev, n_inner, ch_dev),
            "inner",
            split_axis=1,
            concat_axis=0,
            tiled=True,
        ),
        lax.all_to_all(bc_send, "inner", split_axis=1, concat_axis=0, tiled=True),
        lax.all_to_all(dt_send, "inner", split_axis=1, concat_axis=0, tiled=True),
    )
    x_slab = x_recv.reshape(-1, ch_dev)
    bc_slab = bc_recv.reshape(-1, 2 * STATE)
    bias_heads = lax.dynamic_slice_in_dim(dt_bias, inner_idx * heads_dev, heads_dev, 0)
    rate_heads = -jnp.exp(lax.dynamic_slice_in_dim(a_log, inner_idx * heads_dev, heads_dev, 0))
    skip_heads = lax.dynamic_slice_in_dim(d_skip, inner_idx * heads_dev, heads_dev, 0)
    dt_heads = jax.nn.softplus(
        dt_recv.reshape(-1, heads_dev).astype(jnp.float32) + bias_heads[None, :]
    )
    da_heads = dt_heads * rate_heads[None, :]
    c_slab = bc_slab[:, STATE:]
    y_local, end_state = slab_core(x_slab, bc_slab[:, :STATE], c_slab, dt_heads, da_heads)
    cum_slab = jnp.cumsum(da_heads, axis=0)
    slab_decay = head_columns(jnp.exp(cum_slab[-1:]), heads_dev)[0]
    incoming = jnp.zeros_like(end_state)
    outgoing = end_state
    for hop_number in range(n_slab - 1):
        incoming = from_behind(outgoing, "slab", 1)
        outgoing = slab_decay[None, :] * incoming + end_state
    carried = jnp.dot(c_slab, incoming.astype(jnp.bfloat16), preferred_element_type=jnp.float32)
    carried = carried * head_columns(jnp.exp(cum_slab), heads_dev)
    skip_cols = jnp.repeat(skip_heads, HEADDIM)
    y_slab = y_local + carried + skip_cols[None, :] * x_slab.astype(jnp.float32)
    return y_slab.astype(jnp.bfloat16)


def solution(mesh):
    placed = (
        P(("slab", "inner"), None),
        P(("slab", "inner"), None),
        P(("slab", "inner"), None),
        P(),
        P(),
        P(),
        P(),
        P(),
        P(),
        P(),
    )
    return jax.shard_map(
        shards, mesh=mesh, in_specs=placed, out_specs=P("slab", "inner"), check_vma=False
    )
```

profile of v0, /device:TPU:0, one launch (start us, length us, event | category | flops | bytes accessed | tf_op | source)
XLA Modules:
  0.0 606.8 jit_solution(15291614099124217635)
XLA Ops:
  1.7 7.3 %all-to-all-start = ((bf16[256,8,32]{0,2,1:T(8,128)(2,1)}), bf16[256,8,32]{0,2,1:T(8,128)(2,1)S(1)}, u32[]{:S(2)}, u32[]{:S(2)}) async-start(bf16[256,8,32]{0,2,1:T(8,128)(2,1)} %bitcast), calls=%async_computation | async-start | bytes 262144 | tf_op jit(solution)/shard_map/all_to_all | solution.py:126
  9.8 4.5 collective-permute-start
  29.7 7.0 %multiply_convert_fusion.4 = bf16[256,4096]{0,1:T(8,128)(2,1)S(1)} fusion(f32[259,4096]{0,1:T(8,128)S(1)} %maximum_convert_fusion.1, f32[4096]{0:T(1024)S(1)} %bitcast.210, f32[4096]{0:T(1024)S(1)} %bitcast.211, f32[4096]{0:T(1024)S(1)} %bitcast.209, f32[4096]{0:T(1024)S(1)} %bitcast.208, f32[4096]{0:T(1024)S(1)} %copy-done.6), kind=kLoop, calls=%fused_computation.66 | loop fusion | flops 13631488 | bytes 18956288 | tf_op jit(solution)/shard_map/convert_element_type | solution.py:28
  47.0 11.8 %maximum_convert_fusion = f32[259,16384]{1,0:T(8,128)} fusion(bf16[256,16384]{1,0:T(8,128)(2,1)} %param.13, bf16[3,16384]{1,0:T(4,128)(2,1)} %collective-permute-done.1), kind=kLoop, calls=%fused_computation.56 | loop fusion | flops 16973824 | bytes 25460736 | tf_op jit(solution)/shard_map/convert_element_type | solution.py:24
  62.8 27.1 %multiply_convert_fusion.3 = bf16[256,16384]{1,0:T(8,128)(2,1)} fusion(f32[259,16384]{1,0:T(8,128)} %maximum_convert_fusion, f32[16384]{0:T(1024)S(1)} %bitcast.204, f32[16384]{0:T(1024)S(1)} %bitcast.205, f32[16384]{0:T(1024)S(1)} %bitcast.203, f32[16384]{0:T(1024)S(1)} %bitcast.202, f32[16384]{0:T(1024)S(1)} %copy-done.5), kind=kLoop, calls=%fused_computation.55 | loop fusion | flops 54525952 | bytes 75825152 | tf_op jit(solution)/shard_map/convert_element_type | solution.py:28
  89.9 11.9 %copy.96 = bf16[256,16384]{0,1:T(8,128)(2,1)} copy(bf16[256,16384]{1,0:T(8,128)(2,1)} %multiply_convert_fusion.3) | data formatting | bytes 16777216 | tf_op jit(solution)/shard_map/convert_element_type | solution.py:28
  101.9 10.6 %all-to-all-done.1 = bf16[256,8,512]{0,2,1:T(8,128)(2,1)S(1)} async-done(((bf16[256,8,512]{0,2,1:T(8,128)(2,1)}), bf16[256,8,512]{0,2,1:T(8,128)(2,1)S(1)}, u32[]{:S(2)}, u32[]{:S(2)}) %all-to-all-start.1) | async-done | bytes 2097184 | tf_op jit(solution)/shard_map/all_to_all | solution.py:125
  113.7 5.1 all-to-all-start.2
  127.1 175.1 %all-to-all-done.2 = bf16[256,8,2048]{0,2,1:T(8,128)(2,1)} async-done(((bf16[256,8,2048]{0,2,1:T(8,128)(2,1)}), bf16[256,8,2048]{0,2,1:T(8,128)(2,1)}, u32[]{:S(2)}, u32[]{:S(2)}) %all-to-all-start.2) | async-done | bytes 8388640 | tf_op jit(solution)/shard_map/all_to_all | solution.py:118
  302.1 194.8 %while.13 = (s32[]{:T(128)}, f32[256,2048]{1,0:T(8,128)S(1)}, f32[8,256,2048]{2,1,0:T(8,128)}, f32[8,256,32]{1,2,0:T(8,128)}, bf16[8,256,256]{2,1,0:T(8,128)(2,1...) while((s32[]{:T(128)}, f32[256,2048]{1,0:T(8,128)S(1)}, ...), condition=%wide.region_3.4_spmd.clone, body=%wide.region_0.3_spmd.clone.sunk | while | flops 857301120 | bytes 33167368 | solution.py:78
  331.7 4.2 fusion.72
  356.0 4.2 fusion.72
  380.4 4.2 fusion.72
  404.7 4.2 fusion.72
  429.1 4.2 fusion.72
  453.4 4.2 fusion.72
  477.8 4.2 fusion.72
  499.9 9.1 %reduce-window.16 = f32[32,16,128]{2,1,0:T(8,128)S(1)} reduce-window(f32[32,16,128]{2,1,0:T(8,128)S(1)} %bitcast.199, f32[]{:T(128)} %constant.44.clone.1), window={size=1x1x128 pad=0_0x0_0x127_0}, to_apply=%region_4.5 | reduce-window | flops 8323072 | bytes 524292 | tf_op jit(solution)/shard_map/reduce-window.2
  513.4 14.0 %collective-permute-start.3 = (f32[256,2048]{1,0:T(8,128)}, f32[256,2048]{1,0:T(8,128)}, u32[]{:S(2)}, u32[]{:S(2)}) collective-permute-start(f32[256,2048]{1,0:T(8,128)} %multiply_add_fusion.1), channel_id=1, source_target_pairs={{0,8},{8,16},{16,24},{1,9},{9,17},{17,25},{2,10},{10,18},{18,26},{... | collective-permute-start | bytes 6291464 | tf_op jit(solution)/shard_map/ppermute | solution.py:18
  527.7 7.8 %broadcast_in_dim.88 = f32[2048,32,64]{0,2,1:T(8,128)} broadcast(f32[2048,32]{0,1:T(8,128)S(1)} %fusion.47), dimensions={0,1} | broadcast | bytes 17039360 | tf_op jit(solution)/shard_map/broadcast_in_dim | solution.py:33
  535.6 17.6 %copy.100 = f32[2048,2048]{1,0:T(8,128)} copy(f32[2048,2048]{0,1:T(8,128)} %bitcast.189) | data formatting | bytes 33554432 | tf_op jit(solution)/shard_map/reshape | solution.py:33
  559.3 10.6 %bitcast_convert_fusion = f32[8,256,1,2048]{1,3,0,2:T(8,128)} fusion(bf16[256,8,2048]{0,2,1:T(8,128)(2,1)} %all-to-all-done.2), kind=kLoop, calls=%fused_computation.57 | loop fusion | flops 4194304 | bytes 25165824 | tf_op jit(solution)/shard_map/convert_element_type | solution.py:149
  569.9 16.6 %copy.101 = f32[8,256,1,2048]{3,1,0,2:T(8,128)} copy(f32[8,256,1,2048]{1,3,0,2:T(8,128)} %bitcast_convert_fusion) | data formatting | bytes 33554432 | tf_op jit(solution)/shard_map/convert_element_type | solution.py:149
  586.5 20.3 %fusion.31 = bf16[2048,2048]{1,0:T(8,128)(2,1)} fusion(f32[8,256,1,2048]{3,1,0,2:T(8,128)} %copy.101, f32[8,256,2048]{2,1,0:T(8,128)} %get-tuple-element.48, f32[2048,2048]{1,0:T(8,128)} %copy.100, f32[2048]{0:T(1024)S(1)} %mul.208, bf16[256,2048]{1,0:T(8,128)(2,1)S(1)} %collective-permute-done.4, bf16[2048,512]{1,0:T(8,128)(2,1)S(1)} %bitcast.193), kind=kOutput, calls=%fused_computation.53 | convolution fusion | flops 2168455168 | bytes 60825600 | tf_op jit(solution)/shard_map/dot_general | solution.py:146
  (233 shorter events, 220.3 us)
Async XLA Ops:
  1.7 57.1 %all-to-all-start = ((bf16[256,8,32]{0,2,1:T(8,128)(2,1)}), bf16[256,8,32]{0,2,1:T(8,128)(2,1)S(1)}, u32[]{:S(2)}, u32[]{:S(2)}) async-start(bf16[256,8,32]{0,2,1:T(8,128)(2,1)} %bitcast), calls=%async_computation | async-start | bytes 262144 | tf_op jit(solution)/shard_map/all_to_all | solution.py:126
  9.8 17.2 %collective-permute-start = (bf16[3,4096]{1,0:T(4,128)(2,1)S(1)}, bf16[3,4096]{1,0:T(4,128)(2,1)}, u32[]{:S(2)}, u32[]{:S(2)}) collective-permute-start(bf16[3,4096]{1,0:T(4,128)(2,1)S(1)} %slice.80), channel_id=1, source_target_pairs={{0,1},{1,2},{2,3},{3,4},{4,5},{5,6},{6,7},{7,8},{8,9},{9,10},{10,1... | collective-permute-start | bytes 73736 | tf_op jit(solution)/shard_map/ppermute | solution.py:18
  16.0 31.0 %collective-permute-start.1 = (bf16[3,16384]{1,0:T(4,128)(2,1)}, bf16[3,16384]{1,0:T(4,128)(2,1)}, u32[]{:S(2)}, u32[]{:S(2)}) collective-permute-start(bf16[3,16384]{1,0:T(4,128)(2,1)} %slice.90), channel_id=1, source_target_pairs={{0,1},{1,2},{2,3},{3,4},{4,5},{5,6},{6,7},{7,8},{8,9},{9,10},{10,1... | collective-permute-start | bytes 294920 | tf_op jit(solution)/shard_map/ppermute | solution.py:18
  28.3 1.4 copy-start.2
  28.3 1.4 copy-start.3
  28.3 1.4 copy-start.4
  28.3 1.4 copy-start.6
  36.7 4.8 copy-start.7
  58.8 4.0 copy-start.5
  58.8 53.6 %all-to-all-start.1 = ((bf16[256,8,512]{0,2,1:T(8,128)(2,1)}), bf16[256,8,512]{0,2,1:T(8,128)(2,1)S(1)}, u32[]{:S(2)}, u32[]{:S(2)}) async-start(bf16[256,8,512]{0,2,1:T(8,128)(2,1)} %bitcast.195), calls=%async_computation.1 | async-start | bytes 4194304 | tf_op jit(solution)/shard_map/all_to_all | solution.py:125
  112.4 1.3 copy-start.1
  112.4 6.5 %copy-start.8 = (f32[256]{0:T(256)S(1)}, f32[256]{0:T(256)}, u32[]{:S(2)}) copy-start(f32[256]{0:T(256)} %param.16) | copy-start | bytes 3076
  112.4 6.6 %copy-start.9 = (f32[256]{0:T(256)S(1)}, f32[256]{0:T(256)}, u32[]{:S(2)}) copy-start(f32[256]{0:T(256)} %param.17) | copy-start | bytes 3076
  113.7 188.4 %all-to-all-start.2 = ((bf16[256,8,2048]{0,2,1:T(8,128)(2,1)}), bf16[256,8,2048]{0,2,1:T(8,128)(2,1)}, u32[]{:S(2)}, u32[]{:S(2)}) async-start(bf16[256,8,2048]{0,2,1:T(8,128)(2,1)} %bitcast.191), calls=%async_computation.2 | async-start | bytes 16777216 | tf_op jit(solution)/shard_map/all_to_all | solution.py:118
  496.9 13.2 %collective-permute-start.2 = (f32[256,2048]{1,0:T(8,128)S(1)}, f32[256,2048]{1,0:T(8,128)}, u32[]{:S(2)}, u32[]{:S(2)}) collective-permute-start(f32[256,2048]{1,0:T(8,128)S(1)} %get-tuple-element.49), channel_id=1, source_target_pairs={{0,8},{8,16},{16,24},{1,9},{9,17},{17,25},{2,10},{10,18},{18,26},{... | collective-permute-start | bytes 6291464 | tf_op jit(solution)/shard_map/ppermute | solution.py:18
  509.0 18.4 %copy-start.10 = (f32[256]{0:T(256)S(1)}, f32[256]{0:T(256)}, u32[]{:S(2)}) copy-start(f32[256]{0:T(256)} %param.18) | copy-start | bytes 3076
  513.4 39.8 %collective-permute-start.3 = (f32[256,2048]{1,0:T(8,128)}, f32[256,2048]{1,0:T(8,128)}, u32[]{:S(2)}, u32[]{:S(2)}) collective-permute-start(f32[256,2048]{1,0:T(8,128)} %multiply_add_fusion.1), channel_id=1, source_target_pairs={{0,8},{8,16},{16,24},{1,9},{9,17},{17,25},{2,10},{10,18},{18,26},{... | collective-permute-start | bytes 6291464 | tf_op jit(solution)/shard_map/ppermute | solution.py:18
  556.1 30.4 %collective-permute-start.4 = (bf16[256,2048]{1,0:T(8,128)(2,1)}, bf16[256,2048]{1,0:T(8,128)(2,1)S(1)}, u32[]{:S(2)}, u32[]{:S(2)}) collective-permute-start(bf16[256,2048]{1,0:T(8,128)(2,1)} %multiply_add_fusion), channel_id=1, source_target_pairs={{0,8},{8,16},{16,24},{1,9},{9,17},{17,25},{2,10},{10,18},{18,26},{... | collective-permute-start | bytes 3145736 | tf_op jit(solution)/shard_map/ppermute | solution.py:18
  569.9 16.6 %copy-start = (bf16[8,256,1,512]{3,1,0,2:T(8,128)(2,1)S(1)}, bf16[8,256,1,512]{3,1,0,2:T(8,128)(2,1)}, u32[]{:S(2)}) copy-start(bf16[8,256,1,512]{3,1,0,2:T(8,128)(2,1)} %copy.95) | copy-start | bytes 6291460
where the time goes:
time: 611 us; the launch traced here: 607 us
  waiting for transfers between devices  186 us (30%)
  local copies, waits for them, and re-layouts  163 us (27%)
  matrix products  113 us (18%)
  other arithmetic  99.8 us (16%)
  starting transfers between devices  44.3 us (7%)
    all_to_all x1, waiting for transfers between devices, shards(): lax.all_to_all(x_ready.reshape(tok_dev, n_inner, ch_dev), 'inner', split_...  175 us
    reshape x9, local copies, waits for them, and re-layouts, head_columns(): jnp.broadcast_to(per_head[:, :, None], (rows, head_count, HEADDIM))  40.8 us
    convert_element_type x2, other arithmetic, causal_conv(): return jax.nn.silu(summed).astype(jnp.bfloat16)  34.1 us
    dot_general x8, matrix products, span_step(): jnp.einsum('hts,shp->thp', mixing, x_heads, preferred_element_type=jnp.fl...  33.6 us
    dot_general x8, matrix products, span_step(): jnp.dot(c_span, state.astype(jnp.bfloat16), preferred_element_type=jnp.fl...  32.4 us
    ppermute x5, starting transfers between devices, from_behind(): return lax.ppermute(x, axis, pairs)  27.8 us
    reshape x8, local copies, waits for them, and re-layouts, span_step(): y_intra = jnp.einsum('hts,shp->thp', mixing, x_heads, preferred_element_t...  23.5 us
    broadcast_in_dim x27, local copies, waits for them, and re-layouts, head_columns(): jnp.broadcast_to(per_head[:, :, None], (rows, head_count, HEADDIM))  21 us
  transfers between devices with their start and end apart: 8, of which 2 were waited for; matrix products, arithmetic and copies ran while one was open for 25% of the time, Pallas kernels for 0%

commit v1 on v0

--- a/solution.py
+++ b/solution.py
@@ -10,6 +10,9 @@
 GROUPS = 8
 CONV = 4
 SPAN = 256
+group_block = lambda panel: jnp.concatenate(
+    lax.all_to_all(jnp.stack(jnp.split(panel, lax.axis_size("inner"), 1)), "inner", 0, 0), 0
+)
 
 
 def from_behind(x, axis, by):
@@ -115,13 +118,7 @@
     bc_ready = causal_conv(bc_in, bc_prev, conv_bc_weight, conv_bc_bias)
     bc_send = group_copies(bc_ready, dest_group, n_inner)
     x_recv, bc_recv, dt_recv = (
-        lax.all_to_all(
-            x_ready.reshape(tok_dev, n_inner, ch_dev),
-            "inner",
-            split_axis=1,
-            concat_axis=0,
-            tiled=True,
-        ),
+        group_block(x_ready.reshape(tok_dev, n_inner, ch_dev)),
         lax.all_to_all(bc_send, "inner", split_axis=1, concat_axis=0, tiled=True),
         lax.all_to_all(dt_send, "inner", split_axis=1, concat_axis=0, tiled=True),
     )

time: 611 us -> 656 us (1.074)
  waiting for transfers between devices: 186 us -> 213 us
  starting transfers between devices: 44.3 us -> 63.4 us
  other arithmetic: 99.8 us -> 86.2 us
  local copies, waits for them, and re-layouts: 163 us -> 174 us
    all_to_all x1, waiting for transfers between devices: 10.6 us -> 34.9 us  [shards(): lax.all_to_all(bc_send, 'inner', split_axis=1, concat_axis=0, tiled=True)]
    ppermute x5, starting transfers between devices: 27.8 us -> 50.1 us  [from_behind(): return lax.ppermute(x, axis, pairs)]
    unnamed x27 -> x36, local copies, waits for them, and re-layouts: 6.42 us -> 19.4 us
    convert_element_type x1 -> x0, other arithmetic: 10.6 us -> none  [shards(): y_slab = y_local + carried + skip_cols[None, :] * x_slab.astype(jnp.float32)]
  transfers between devices with their start and end apart: 8 -> 8, of which waited for: 2 -> 3; matrix products, arithmetic and copies ran while one was open for 25% -> 23% of each run, Pallas kernels for 0% -> 0%
where the time goes in v1:
time: 656 us; the launch traced here: 651 us
  waiting for transfers between devices  213 us (32%)
  local copies, waits for them, and re-layouts  174 us (27%)
  matrix products  114 us (17%)
  other arithmetic  86.2 us (13%)
  starting transfers between devices  63.4 us (10%)
    all_to_all x1, waiting for transfers between devices, lax.all_to_all(jnp.stack(jnp.split(panel, lax.axis_size('inner'), 1)), 'i...  175 us
    ppermute x5, starting transfers between devices, from_behind(): return lax.ppermute(x, axis, pairs)  50.1 us
    reshape x9, local copies, waits for them, and re-layouts, head_columns(): jnp.broadcast_to(per_head[:, :, None], (rows, head_count, HEADDIM))  40.8 us
    all_to_all x1, waiting for transfers between devices, shards(): lax.all_to_all(bc_send, 'inner', split_axis=1, concat_axis=0, tiled=True)  34.9 us
    convert_element_type x2, other arithmetic, causal_conv(): return jax.nn.silu(summed).astype(jnp.bfloat16)  34.1 us
    dot_general x8, matrix products, span_step(): jnp.einsum('hts,shp->thp', mixing, x_heads, preferred_element_type=jnp.fl...  33.6 us
    dot_general x8, matrix products, span_step(): jnp.dot(c_span, state.astype(jnp.bfloat16), preferred_element_type=jnp.fl...  32.4 us
    reshape x8, local copies, waits for them, and re-layouts, span_step(): y_intra = jnp.einsum('hts,shp->thp', mixing, x_heads, preferred_element_t...  23.5 us
  transfers between devices with their start and end apart: 8, of which 3 were waited for; matrix products, arithmetic and copies ran while one was open for 23% of the time, Pallas kernels for 0%

profile of v1, /device:TPU:0, one launch (start us, length us, event | category | flops | bytes accessed | tf_op | source)
XLA Modules:
  0.0 650.8 jit_solution(14489552291728759186)
XLA Ops:
  1.7 5.5 collective-permute-start.1
  8.8 4.2 all-to-all-start
  13.9 4.5 collective-permute-start
  28.9 7.0 %multiply_convert_fusion.4 = bf16[256,4096]{0,1:T(8,128)(2,1)S(1)} fusion(f32[259,4096]{0,1:T(8,128)S(1)} %maximum_convert_fusion.1, f32[4096]{0:T(1024)S(1)} %bitcast.244, f32[4096]{0:T(1024)S(1)} %bitcast.245, f32[4096]{0:T(1024)S(1)} %bitcast.243, f32[4096]{0:T(1024)S(1)} %bitcast.242, f32[4096]{0:T(1024)S(1)} %copy-done.7), kind=kLoop, calls=%fused_computation.65 | loop fusion | flops 13631488 | bytes 18956288 | tf_op jit(solution)/shard_map/convert_element_type | solution.py:31
  46.2 11.8 %maximum_convert_fusion = f32[259,16384]{1,0:T(8,128)} fusion(bf16[256,16384]{1,0:T(8,128)(2,1)} %param.13, bf16[3,16384]{1,0:T(4,128)(2,1)} %collective-permute-done.1), kind=kLoop, calls=%fused_computation.56 | loop fusion | flops 16973824 | bytes 25460736 | tf_op jit(solution)/shard_map/convert_element_type | solution.py:27
  58.0 27.1 %multiply_convert_fusion.3 = bf16[256,16384]{1,0:T(8,128)(2,1)} fusion(f32[259,16384]{1,0:T(8,128)} %maximum_convert_fusion, f32[16384]{0:T(1024)S(1)} %bitcast.238, f32[16384]{0:T(1024)S(1)} %bitcast.239, f32[16384]{0:T(1024)S(1)} %bitcast.237, f32[16384]{0:T(1024)S(1)} %bitcast.236, f32[16384]{0:T(1024)S(1)} %copy-done.6), kind=kLoop, calls=%fused_computation.55 | loop fusion | flops 54525952 | bytes 75825152 | tf_op jit(solution)/shard_map/convert_element_type | solution.py:31
  85.1 12.0 %copy.117 = bf16[256,16384]{0,1:T(8,128)(2,1)} copy(bf16[256,16384]{1,0:T(8,128)(2,1)} %multiply_convert_fusion.3) | data formatting | bytes 16777216 | tf_op jit(solution)/shard_map/convert_element_type | solution.py:31
  115.1 34.9 %all-to-all-done.1 = bf16[256,8,512]{0,2,1:T(8,128)(2,1)S(1)} async-done(((bf16[256,8,512]{0,2,1:T(8,128)(2,1)}), bf16[256,8,512]{0,2,1:T(8,128)(2,1)S(1)}, u32[]{:S(2)}, u32[]{:S(2)}) %all-to-all-start.1) | async-done | bytes 2097184 | tf_op jit(solution)/shard_map/all_to_all | solution.py:122
  151.3 5.1 all-to-all-start.2
  164.6 174.5 %all-to-all-done.2 = bf16[8,256,1,2048]{1,3,2,0:T(8,128)(2,1)} async-done(((bf16[8,256,1,2048]{1,3,2,0:T(8,128)(2,1)}), bf16[8,256,1,2048]{1,3,2,0:T(8,128)(2,1)}, u32[]{:S(2)}, u32[]{:S(2)}) %all-to-all-start.2) | async-done | bytes 8388640 | tf_op jit(solution)/shard_map/all_to_all | solution.py:14
  339.2 194.7 %while.13 = (s32[]{:T(128)}, f32[256,2048]{1,0:T(8,128)S(1)}, f32[8,256,2048]{2,1,0:T(8,128)}, f32[8,256,32]{1,2,0:T(8,128)}, bf16[8,256,256]{2,1,0:T(8,128)(2,1...) while((s32[]{:T(128)}, f32[256,2048]{1,0:T(8,128)S(1)}, ...), condition=%wide.region_3.4_spmd.clone, body=%wide.region_0.3_spmd.clone.sunk | while | flops 857301120 | bytes 33167368 | solution.py:81
  368.7 4.2 fusion.80
  393.0 4.2 fusion.80
  417.4 4.2 fusion.80
  441.7 4.2 fusion.80
  490.4 4.2 fusion.80
  514.8 4.2 fusion.80
  536.8 9.1 %reduce-window.16 = f32[32,16,128]{2,1,0:T(8,128)S(1)} reduce-window(f32[32,16,128]{2,1,0:T(8,128)S(1)} %bitcast.233, f32[]{:T(128)} %constant.44.clone.1), window={size=1x1x128 pad=0_0x0_0x127_0}, to_apply=%region_4.5 | reduce-window | flops 8323072 | bytes 524292 | tf_op jit(solution)/shard_map/reduce-window.2
  549.0 12.8 %collective-permute-start.3 = (f32[256,2048]{1,0:T(8,128)S(1)}, f32[256,2048]{1,0:T(8,128)S(1)}, u32[]{:S(2)}, u32[]{:S(2)}) collective-permute-start(f32[256,2048]{1,0:T(8,128)S(1)} %multiply_add_fusion.1), channel_id=1, source_target_pairs={{0,8},{8,16},{16,24},{1,9},{9,17},{17,25},{2,10},{10,18},{18,26},{... | collective-permute-start | bytes 6291464 | tf_op jit(solution)/shard_map/ppermute | solution.py:21
  566.8 24.7 %collective-permute-start.4 = (bf16[256,2048]{1,0:T(8,128)(2,1)}, bf16[256,2048]{1,0:T(8,128)(2,1)}, u32[]{:S(2)}, u32[]{:S(2)}) collective-permute-start(bf16[256,2048]{1,0:T(8,128)(2,1)} %multiply_add_fusion), channel_id=1, source_target_pairs={{0,8},{8,16},{16,24},{1,9},{9,17},{17,25},{2,10},{10,18},{18,26},{... | collective-permute-start | bytes 3145736 | tf_op jit(solution)/shard_map/ppermute | solution.py:21
  591.7 7.9 %broadcast_in_dim.88 = f32[2048,32,64]{0,2,1:T(8,128)} broadcast(f32[2048,32]{0,1:T(8,128)S(1)} %fusion.55), dimensions={0,1} | broadcast | bytes 17039360 | tf_op jit(solution)/shard_map/broadcast_in_dim | solution.py:36
  599.6 17.7 %copy.121 = f32[2048,2048]{1,0:T(8,128)} copy(f32[2048,2048]{0,1:T(8,128)} %bitcast.216) | data formatting | bytes 33554432 | tf_op jit(solution)/shard_map/reshape | solution.py:36
  617.3 12.9 %copy.122 = f32[8,256,1,2048]{3,1,0,2:T(8,128)} copy(bf16[8,256,1,2048]{1,3,2,0:T(8,128)(2,1)} %all-to-all-done.2) | data formatting | bytes 25165824 | tf_op jit(solution)/shard_map/convert_element_type | solution.py:146
  630.2 20.6 %fusion.31 = bf16[2048,2048]{1,0:T(8,128)(2,1)} fusion(f32[8,256,1,2048]{3,1,0,2:T(8,128)} %copy.122, f32[8,256,2048]{2,1,0:T(8,128)} %get-tuple-element.48, f32[2048,2048]{1,0:T(8,128)} %copy.121, f32[2048]{0:T(1024)S(1)} %mul.208, bf16[256,2048]{1,0:T(8,128)(2,1)} %collective-permute-done.4, bf16[2048,512]{1,0:T(8,128)(2,1)S(1)} %bitcast.227), kind=kOutput, calls=%fused_computation.53 | convolution fusion | flops 2168455168 | bytes 60825600 | tf_op jit(solution)/shard_map/dot_general | solution.py:143
  (242 shorter events, 232.6 us)
Async XLA Ops:
  1.7 44.5 %collective-permute-start.1 = (bf16[3,16384]{1,0:T(4,128)(2,1)}, bf16[3,16384]{1,0:T(4,128)(2,1)}, u32[]{:S(2)}, u32[]{:S(2)}) collective-permute-start(bf16[3,16384]{1,0:T(4,128)(2,1)} %slice.90), channel_id=1, source_target_pairs={{0,1},{1,2},{2,3},{3,4},{4,5},{5,6},{6,7},{7,8},{8,9},{9,10},{10,1... | collective-permute-start | bytes 294920 | tf_op jit(solution)/shard_map/ppermute | solution.py:21
  8.8 88.3 %all-to-all-start = ((bf16[256,8,32]{0,2,1:T(8,128)(2,1)}), bf16[256,8,32]{0,2,1:T(8,128)(2,1)S(1)}, u32[]{:S(2)}, u32[]{:S(2)}) async-start(bf16[256,8,32]{0,2,1:T(8,128)(2,1)} %bitcast), calls=%async_computation | async-start | bytes 262144 | tf_op jit(solution)/shard_map/all_to_all | solution.py:123
  13.9 12.3 %collective-permute-start = (bf16[3,4096]{1,0:T(4,128)(2,1)S(1)}, bf16[3,4096]{1,0:T(4,128)(2,1)}, u32[]{:S(2)}, u32[]{:S(2)}) collective-permute-start(bf16[3,4096]{1,0:T(4,128)(2,1)S(1)} %slice.80), channel_id=1, source_target_pairs={{0,1},{1,2},{2,3},{3,4},{4,5},{5,6},{6,7},{7,8},{8,9},{9,10},{10,1... | collective-permute-start | bytes 73736 | tf_op jit(solution)/shard_map/ppermute | solution.py:21
  27.5 1.4 copy-start.3
  27.5 1.4 copy-start.4
  27.5 1.4 copy-start.5
  27.5 1.4 copy-start.7
  35.9 4.8 copy-start.8
  46.2 11.8 %copy-start.6 = (f32[16384]{0:T(1024)S(1)}, f32[16384]{0:T(1024)}, u32[]{:S(2)}) copy-start(f32[16384]{0:T(1024)} %param.20) | copy-start | bytes 196612
  97.1 52.9 %all-to-all-start.1 = ((bf16[256,8,512]{0,2,1:T(8,128)(2,1)}), bf16[256,8,512]{0,2,1:T(8,128)(2,1)S(1)}, u32[]{:S(2)}, u32[]{:S(2)}) async-start(bf16[256,8,512]{0,2,1:T(8,128)(2,1)} %bitcast.229), calls=%async_computation.1 | async-start | bytes 4194304 | tf_op jit(solution)/shard_map/all_to_all | solution.py:122
  101.1 9.9 %copy-start = (bf16[256,16384]{0,1:T(8,128)(2,1)S(1)}, bf16[256,16384]{0,1:T(8,128)(2,1)}, u32[]{:S(2)}) copy-start(bf16[256,16384]{0,1:T(8,128)(2,1)} %copy.117) | copy-start | bytes 25165828
  115.1 41.4 %copy-start.9 = (f32[256]{0:T(256)S(1)}, f32[256]{0:T(256)}, u32[]{:S(2)}) copy-start(f32[256]{0:T(256)} %param.16) | copy-start | bytes 3076
  115.1 41.5 %copy-start.10 = (f32[256]{0:T(256)S(1)}, f32[256]{0:T(256)}, u32[]{:S(2)}) copy-start(f32[256]{0:T(256)} %param.17) | copy-start | bytes 3076
  150.0 1.3 copy-start.2
  151.3 187.8 %all-to-all-start.2 = ((bf16[8,256,1,2048]{1,3,2,0:T(8,128)(2,1)}), bf16[8,256,1,2048]{1,3,2,0:T(8,128)(2,1)}, u32[]{:S(2)}, u32[]{:S(2)}) async-start(bf16[8,256,1,2048]{1,3,2,0:T(8,128)(2,1)} %fusion.36), calls=%async_computation.2 | async-start | bytes 16777216 | tf_op jit(solution)/shard_map/all_to_all | solution.py:14
  533.9 57.6 %copy-start.11 = (f32[256]{0:T(256)S(1)}, f32[256]{0:T(256)}, u32[]{:S(2)}) copy-start(f32[256]{0:T(256)} %param.18) | copy-start | bytes 3076
  533.9 13.2 %collective-permute-start.2 = (f32[256,2048]{1,0:T(8,128)S(1)}, f32[256,2048]{1,0:T(8,128)}, u32[]{:S(2)}, u32[]{:S(2)}) collective-permute-start(f32[256,2048]{1,0:T(8,128)S(1)} %get-tuple-element.49), channel_id=1, source_target_pairs={{0,8},{8,16},{16,24},{1,9},{9,17},{17,25},{2,10},{10,18},{18,26},{... | collective-permute-start | bytes 6291464 | tf_op jit(solution)/shard_map/ppermute | solution.py:21
  549.0 16.4 %collective-permute-start.3 = (f32[256,2048]{1,0:T(8,128)S(1)}, f32[256,2048]{1,0:T(8,128)S(1)}, u32[]{:S(2)}, u32[]{:S(2)}) collective-permute-start(f32[256,2048]{1,0:T(8,128)S(1)} %multiply_add_fusion.1), channel_id=1, source_target_pairs={{0,8},{8,16},{16,24},{1,9},{9,17},{17,25},{2,10},{10,18},{18,26},{... | collective-permute-start | bytes 6291464 | tf_op jit(solution)/shard_map/ppermute | solution.py:21
  566.8 63.5 %collective-permute-start.4 = (bf16[256,2048]{1,0:T(8,128)(2,1)}, bf16[256,2048]{1,0:T(8,128)(2,1)}, u32[]{:S(2)}, u32[]{:S(2)}) collective-permute-start(bf16[256,2048]{1,0:T(8,128)(2,1)} %multiply_add_fusion), channel_id=1, source_target_pairs={{0,8},{8,16},{16,24},{1,9},{9,17},{17,25},{2,10},{10,18},{18,26},{... | collective-permute-start | bytes 3145736 | tf_op jit(solution)/shard_map/ppermute | solution.py:21
  617.3 13.0 %copy-start.1 = (bf16[8,256,1,512]{3,1,0,2:T(8,128)(2,1)S(1)}, bf16[8,256,1,512]{3,1,0,2:T(8,128)(2,1)}, u32[]{:S(2)}) copy-start(bf16[8,256,1,512]{3,1,0,2:T(8,128)(2,1)} %copy.116) | copy-start | bytes 6291460
